TPU v7x, 256 devices: a whole 4x4x8 slice. The times are simulated.
256 devices in a mesh: context: 16 (over z, core), heads: 16 (over x, y).
Axes of the slice: x: 4, y: 4, z: 8, core: 2. Of those that a mesh axis runs over, the one named last changes fastest.
Arguments:
- main_query: bfloat16 [256, 128, 576], P('context', 'heads'), may hold values from -6 to 6
- latent_keys: bfloat16 [32768, 576], P('context'), may hold values from -6 to 6
- head_lse: float32 [256, 128], P(None, 'heads'), may hold values from 4 to 8
- lengths: int32 [256], replicated, may hold values from 1 to 32768, as said below
- index_query: bfloat16 [256, 64, 128], P('heads'), may hold values from -256 to 256
- index_key: bfloat16 [32768, 128], P('context'), may hold values from -8 to 8
- index_weight: float32 [256, 64], P('heads'), may hold values from -2.4 to 2.4
Outputs:
- grad_index_query: float32 [256, 64, 128], P('heads', 'context')
- grad_index_key: float32 [32768, 128], P(('context', 'heads'))
Inputs may be any that keep to these rules, and one draw needn't show every extreme that they name: Query rows come in blocks of 16 consecutive rows whose lengths rise by one from row to row; some block ends at the last key.
All inputs are finite; a program needn't handle non-finite values.
Results may differ from a plain program's by a relative error of at most 0.0029.
Values may be sent and summed in bfloat16 or wider, within the bound.
A program may use at most 64 MiB of HBM per device.

v0:
```python
import math
import jax
import jax.numpy as jnp
from jax import lax
from jax.sharding import PartitionSpec as P

main_scale = 192.0 ** (-0.5)
loss_scale = 64.0
masked_low = -1e30


def head_mass(queries, lse_rows, len_rows, latent, first_key):
    row_count = queries.shape[0]
    block_rows = math.gcd(row_count, 64)
    steps_count = row_count // block_rows
    key_pos = first_key + jnp.arange(latent.shape[0], dtype=jnp.int32)

    def one_block(inputs):
        query_block, lse_block, len_block = inputs
        scores = (
            jnp.einsum("rhd,sd->rhs", query_block, latent, preferred_element_type=jnp.float32)
            * main_scale
        )
        summed = jnp.sum(jnp.exp(scores - lse_block[:, :, None]), axis=1)
        return jnp.where(key_pos[None, :] < len_block[:, None], summed, 0.0)

    stacked = lax.map(
        one_block,
        (
            queries.reshape((steps_count, block_rows) + queries.shape[1:]),
            lse_rows.reshape(steps_count, block_rows, lse_rows.shape[1]),
            len_rows.reshape(steps_count, block_rows),
        ),
    )
    return stacked.reshape(row_count, latent.shape[0])


def on_device(main_query, latent_keys, head_lse, lengths, index_query, index_key, index_weight):
    key_count = latent_keys.shape[0]
    first_key = lax.axis_index("context") * key_count
    own_rows = index_query.shape[0]
    row_first = lax.axis_index("heads") * own_rows
    partial_mass = head_mass(
        lax.all_gather(main_query, "context", axis=0, tiled=True),
        head_lse,
        lengths,
        latent_keys,
        first_key,
    )
    summed_mass = lax.psum(partial_mass, "heads")
    row_mass = lax.dynamic_slice_in_dim(summed_mass, row_first, own_rows, 0)
    own_len = lax.dynamic_slice_in_dim(lengths, row_first, own_rows, 0)
    visible = (first_key + jnp.arange(key_count, dtype=jnp.int32))[None, :] < own_len[:, None]
    heads_count = index_query.shape[1]
    width = index_query.shape[2]
    index_scale = width ** (-0.5)
    flat_query = index_query.reshape(own_rows * heads_count, width)
    block_keys = math.gcd(key_count, 512)
    block_total = key_count // block_keys
    key_blocks = index_key.reshape(block_total, block_keys, width)

    def block_dots(key_block):
        products = lax.dot_general(
            flat_query, key_block, (((1,), (1,)), ((), ())), preferred_element_type=jnp.float32
        )
        return products.reshape(own_rows, heads_count, key_block.shape[0])

    def block_logits(key_block):
        return (
            jnp.einsum(
                "tj,tjs->ts",
                index_weight,
                jax.nn.relu(block_dots(key_block)),
                precision=lax.Precision.HIGHEST,
            )
            * index_scale
        )

    logits = jnp.moveaxis(lax.map(block_logits, key_blocks), 0, 1).reshape(own_rows, key_count)
    local_top = jnp.max(jnp.where(visible, logits, masked_low), axis=1)
    mass_local = jnp.sum(row_mass, axis=1)
    top = lax.pmax(local_top, "context")
    weights_exp = jnp.where(visible, jnp.exp(logits - top[:, None]), 0.0)
    share_sum, mass_total = lax.psum((jnp.sum(weights_exp, axis=1), mass_local), "context")
    probability = weights_exp / share_sum[:, None]
    target = row_mass / mass_total[:, None]
    slopes = loss_scale * (probability - target)
    slope_blocks = slopes.reshape(own_rows, block_total, block_keys).transpose(1, 0, 2)

    def back_step(query_grad, inputs):
        key_block, slope_block = inputs
        products = block_dots(key_block)
        terms = jnp.where(
            products > 0, slope_block[:, None, :] * index_weight[:, :, None] * index_scale, 0.0
        )
        terms = terms.astype(jnp.bfloat16).reshape(own_rows * heads_count, key_block.shape[0])
        query_grad = query_grad + jnp.dot(terms, key_block, preferred_element_type=jnp.float32)
        key_grad = lax.dot_general(
            terms, flat_query, (((0,), (0,)), ((), ())), preferred_element_type=jnp.float32
        )
        return (query_grad, key_grad)

    start_grad = jnp.zeros((own_rows * heads_count, width), jnp.float32)
    query_grad, key_grads = lax.scan(back_step, start_grad, (key_blocks, slope_blocks))
    query_grad = query_grad.reshape(own_rows, heads_count, width)
    key_grad = key_grads.reshape(key_count, width)
    out_query = lax.psum_scatter(query_grad, "context", scatter_dimension=1, tiled=True)
    out_key = lax.psum_scatter(key_grad, "heads", scatter_dimension=0, tiled=True)
    return (out_query, out_key)


def solution(mesh):
    placed = (
        P("context", "heads", None),
        P("context", None),
        P(None, "heads"),
        P(),
        P("heads", None, None),
        P("context", None),
        P("heads", None),
    )
    return jax.shard_map(
        on_device,
        mesh=mesh,
        in_specs=placed,
        out_specs=(P("heads", "context", None), P(("context", "heads"), None)),
        check_vma=False,
    )
```

profile of v0, /device:TPU:2, one launch (start us, length us, event | category | flops | bytes accessed | tf_op | source)
XLA Modules:
  0.0 374.9 jit_solution(15053279912884742428)
XLA Ops:
  7.2 0.7 all-gather.2.cloned.1.call-update
  8.0 0.8 reshape.139
  8.8 0.8 dynamic_slice.31
  9.5 0.8 copy.25
  10.3 0.8 mul.63
  11.1 41.8 %all-gather.2.cloned.1.call-done = bf16[256,8,576]{2,1,0:T(8,128)(2,1)} async-done(((bf16[16,8,576]{2,1,0:T(8,128)(2,1)}), bf16[256,8,576]{2,1,0:T(8,128)(2,1)}) %all-gather.2.cloned.1.call-update) | async-done | bytes 2359312 | tf_op jit(solution)/shard_map/all_gather | solution.py:44
  52.9 22.9 %while.36 = (s32[]{:T(128)}, f32[4,64,2048]{2,1,0:T(8,128)}, s32[4,64]{1,0:T(4,128)S(1)}, bf16[4,64,8,576]{3,2,1,0:T(8,128)(2,1)}, bf16[2048,576]{0,1:T(8,128)(2...) while((s32[]{:T(128)}, f32[4,64,2048]{2,1,0:T(8,128)}, s32[4,64]{1,0:T(4,128)S(1)}, ...), condition=%wide.region_8.9_spmd.clone, body=%wide.region_6.8_spmd.clone.sunk | while | flops 1211238400 | bytes 4611937 | solution.py:27
  52.9 4.8 %exponential_reduce_fusion.2 = f32[64,2048]{1,0:T(8,128)S(1)} fusion(bf16[2048,576]{0,1:T(8,128)(2,1)} %get-tuple-element.382, f32[64,8]{1,0:T(8,128)S(1)} %dynamic-slice_bitcast_fusion.5, bf16[4,64,8,576]{3,2,1,0:T(8,128)(2,1)} %get-tuple-element.381, s32[]{:T(128)} %get-tuple-element.370), kind=kOutput, calls=%fused_computation.7.clone.1 | convolution fusion | flops 1210974208 | bytes 3541504 | tf_op jit(solution)/shard_map/while/body/eval_jaxpr/rhd,sd->rhs/dot_general | solution.py:21
  57.7 0.9 fusion.60
  58.6 4.8 %exponential_reduce_fusion.2 = f32[64,2048]{1,0:T(8,128)S(1)} fusion(bf16[2048,576]{0,1:T(8,128)(2,1)} %get-tuple-element.382, f32[64,8]{1,0:T(8,128)S(1)} %dynamic-slice_bitcast_fusion.5, bf16[4,64,8,576]{3,2,1,0:T(8,128)(2,1)} %get-tuple-element.381, s32[]{:T(128)} %get-tuple-element.370), kind=kOutput, calls=%fused_computation.7.clone.1 | convolution fusion | flops 1210974208 | bytes 3541504 | tf_op jit(solution)/shard_map/while/body/eval_jaxpr/rhd,sd->rhs/dot_general | solution.py:21
  63.4 0.9 fusion.60
  64.3 4.8 %exponential_reduce_fusion.2 = f32[64,2048]{1,0:T(8,128)S(1)} fusion(bf16[2048,576]{0,1:T(8,128)(2,1)} %get-tuple-element.382, f32[64,8]{1,0:T(8,128)S(1)} %dynamic-slice_bitcast_fusion.5, bf16[4,64,8,576]{3,2,1,0:T(8,128)(2,1)} %get-tuple-element.381, s32[]{:T(128)} %get-tuple-element.370), kind=kOutput, calls=%fused_computation.7.clone.1 | convolution fusion | flops 1210974208 | bytes 3541504 | tf_op jit(solution)/shard_map/while/body/eval_jaxpr/rhd,sd->rhs/dot_general | solution.py:21
  69.1 0.9 fusion.60
  70.0 4.8 %exponential_reduce_fusion.2 = f32[64,2048]{1,0:T(8,128)S(1)} fusion(bf16[2048,576]{0,1:T(8,128)(2,1)} %get-tuple-element.382, f32[64,8]{1,0:T(8,128)S(1)} %dynamic-slice_bitcast_fusion.5, bf16[4,64,8,576]{3,2,1,0:T(8,128)(2,1)} %get-tuple-element.381, s32[]{:T(128)} %get-tuple-element.370), kind=kOutput, calls=%fused_computation.7.clone.1 | convolution fusion | flops 1210974208 | bytes 3541504 | tf_op jit(solution)/shard_map/while/body/eval_jaxpr/rhd,sd->rhs/dot_general | solution.py:21
  74.8 0.9 fusion.60
  75.8 0.9 copy-done
  76.9 19.8 %while.35 = (s32[]{:T(128)}, f32[4,16,512]{2,1,0:T(8,128)S(1)}, bf16[4,512,128]{2,1,0:T(8,128)(2,1)S(1)}, bf16[1024,128]{1,0:T(8,128)(2,1)S(1)}, f32[16,64]{1,0:T(8,128)S(1)}, /*index=5*/s32[]{:T(128)}) while((s32[]{:T(128)}, f32[4,16,512]{2,1,0:T(8,128)S(1)}, bf16[4,512,128]{2,1,0:T(8,128)(2,1)S(1)}, bf16[1024,128]{1,0:T(8,128)(2,1)S(1)}, ...), condition=%wide.region_1.2_spmd, body=%wide.region_0.1_spmd.sunk | while | flops 141041664 | bytes 8884301 | solution.py:79
  76.9 1.8 maximum_bitcast_fusion.2
  78.7 1.9 copy.41
  80.6 1.2 fusion.56
  81.8 1.8 maximum_bitcast_fusion.2
  83.6 1.9 copy.41
  85.6 1.2 fusion.56
  86.8 1.8 maximum_bitcast_fusion.2
  88.6 1.9 copy.41
  90.5 1.2 fusion.56
  91.8 1.8 maximum_bitcast_fusion.2
  93.6 1.9 copy.41
  95.5 1.2 fusion.56
  97.0 24.9 %pmax.7 = f32[16]{0:T(128)S(1)} all-reduce(f32[16]{0:T(128)S(1)} %fusion.18), channel_id=1, replica_groups=mesh['context'=16,'heads'=16] {'context'}, use_global_device_ids=true, to_apply=%region_3.4 | all-reduce | flops 16 | bytes 128 | tf_op jit(solution)/shard_map/pmax | solution.py:82
  122.1 53.3 %all-reduce.3.cloned.1.call-done = f32[256,2048]{1,0:T(8,128)} async-done(((f32[256,2048]{1,0:T(8,128)}), f32[256,2048]{1,0:T(8,128)}) %all-reduce.3.cloned.1.call-update) | async-done | bytes 2097168 | tf_op jit(solution)/shard_map/psum | solution.py:50
  175.4 1.0 dynamic-slice_reduce_fusion
  176.4 24.2 %all-reduce = (f32[16]{0:T(128)S(1)}, f32[16]{0:T(128)S(1)}) all-reduce(f32[16]{0:T(128)S(1)} %dynamic-slice_reduce_fusion, f32[16]{0:T(128)S(1)} %fusion.19), channel_id=1, replica_groups=mesh['context'=16,'heads'=16] {'context'}, use_global_device_ids=true, to_apply=%region_11.12 | all-reduce | flops 32 | bytes 256 | tf_op jit(solution)/shard_map/psum | solution.py:84
  200.6 1.0 subtract_multiply_fusion
  201.6 0.7 copy.35
  202.3 26.9 %while.37 = (s32[]{:T(128)}, f32[1024,128]{1,0:T(8,128)S(1)}, f32[4,512,128]{2,1,0:T(8,128)}, bf16[4,512,128]{2,1,0:T(8,128)(2,1)S(1)}, bf16[1024,128]{1,0:T(8,1...) while((s32[]{:T(128)}, f32[1024,128]{1,0:T(8,128)S(1)}, ...), condition=%wide.wide.region_13.14_spmd.clone, body=%wide.wide.region_12.13_spmd.clone.sunk | while | flops 405536768 | bytes 13734523 | solution.py:104
  202.3 0.8 dynamic-slice_bitcast_fusion.6
  203.1 0.2 mul.80
  203.3 1.8 copy.42
  205.2 2.1 select_convert_fusion.3
  207.3 0.6 convolution_add_fusion.3
  207.9 1.1 fusion.67
  209.0 0.8 dynamic-slice_bitcast_fusion.6
  209.8 0.2 mul.80
  210.0 1.8 copy.42
  211.9 2.1 select_convert_fusion.3
  214.0 0.6 convolution_add_fusion.3
  214.6 1.1 fusion.67
  215.8 0.8 dynamic-slice_bitcast_fusion.6
  216.5 0.2 mul.80
  216.8 1.8 copy.42
  218.6 2.1 select_convert_fusion.3
  220.7 0.6 convolution_add_fusion.3
  221.3 1.1 fusion.67
  222.5 0.8 dynamic-slice_bitcast_fusion.6
  223.5 1.8 copy.42
  225.3 2.1 select_convert_fusion.3
  227.4 0.6 convolution_add_fusion.3
  228.1 1.2 fusion.67
  229.2 1.1 copy.27
  230.4 0.5 reduce-scatter.5.cloned.1.call-update
  231.0 56.1 %reduce-scatter.3.cloned.1.call-done = f32[16,4,128]{2,0,1:T(8,128)} async-done(((f32[16,64,128]{2,0,1:T(8,128)}), f32[16,4,128]{2,0,1:T(8,128)}) %reduce-scatter.3.cloned.1.call-update) | async-done | bytes 32784 | tf_op jit(solution)/shard_map/reduce_scatter | solution.py:107
  287.1 1.4 copy.28
  288.5 79.9 %reduce-scatter.5.cloned.1.call-done = f32[128,128]{1,0:T(8,128)} async-done(((f32[2048,128]{1,0:T(8,128)}), f32[128,128]{1,0:T(8,128)}) %reduce-scatter.5.cloned.1.call-update) | async-done | bytes 65552 | tf_op jit(solution)/shard_map/reduce_scatter | solution.py:108
  (37 shorter events, 1.2 us)
Async XLA Ops:
  7.2 45.7 %all-gather.2.cloned.1.call-start = ((), (), s32[]{:S(2)}) async-start(), calls=%async_computation.2 | async-start | bytes 2785280 | tf_op jit(solution)/shard_map/all_gather | solution.py:44
  7.9 167.5 %all-reduce.3.cloned.1.call-start = ((), (), s32[]{:S(2)}) async-start(), calls=%async_computation.3 | async-start | bytes 4194304 | tf_op jit(solution)/shard_map/psum | solution.py:50
  75.8 0.9 copy-start
  75.8 1.1 copy-start.1
  75.8 1.1 copy-start.2
  75.8 211.3 %reduce-scatter.3.cloned.1.call-start = ((), (), s32[]{:S(2)}) async-start(), calls=%async_computation.4 | async-start | bytes 557056 | tf_op jit(solution)/shard_map/reduce_scatter | solution.py:107
  230.4 138.0 %reduce-scatter.5.cloned.1.call-start = ((), (), s32[]{:S(2)}) async-start(), calls=%async_computation.5 | async-start | bytes 1114112 | tf_op jit(solution)/shard_map/reduce_scatter | solution.py:108
Sparse Core Ops, SparseCore 0:
  9.8 43.0 all-gather.1
  75.9 99.3 all-reduce.2
  230.5 56.5 reduce-scatter.2
  291.0 77.3 reduce-scatter.4
where the time goes:
time: 376 us; the launch traced here: 375 us
  waiting for transfers between devices  232 us (62%)
  blocking collectives  49.1 us (13%)
  matrix products  46.5 us (12%)
  local copies, waits for them, and re-layouts  26.4 us (7%)
  between operations  13.8 us (4%)
  other arithmetic  6.2 us (2%)
    reduce_scatter x1, waiting for transfers between devices, on_device(): lax.psum_scatter(key_grad, 'heads', scatter_dimension=0, tiled=True)  79.9 us
    reduce_scatter x1, waiting for transfers between devices, on_device(): lax.psum_scatter(query_grad, 'context', scatter_dimension=1, tiled=True)  56.1 us
    psum x1, waiting for transfers between devices, on_device(): summed_mass = lax.psum(partial_mass, 'heads')  53.3 us
    all_gather x1, waiting for transfers between devices, on_device(): lax.all_gather(main_query, 'context', axis=0, tiled=True)  41.8 us
    pmax x1, blocking collectives, on_device(): top = lax.pmax(local_top, 'context')  24.9 us
    psum x1, blocking collectives, on_device(): lax.psum((jnp.sum(weights_exp, axis=1), mass_local), 'context')  24.2 us
    dot_general x4, matrix products, one_block(): jnp.einsum('rhd,sd->rhs', query_block, latent, preferred_element_type=jnp...  19 us
    dot_general x8, matrix products, block_dots(): lax.dot_general(flat_query, key_block, (((1,), (1,)), ((), ())), preferre...  15.5 us
  transfers between devices with their start and end apart: 4, of which 4 were waited for; matrix products, arithmetic and copies ran while one was open for 7% of the time, Pallas kernels for 0%

commit v1 on v0

--- a/solution.py
+++ b/solution.py
@@ -47,7 +47,7 @@
         latent_keys,
         first_key,
     )
-    summed_mass = lax.psum(partial_mass, "heads")
+    summed_mass = jnp.sum(lax.all_gather(partial_mass, "heads"), axis=0)
     row_mass = lax.dynamic_slice_in_dim(summed_mass, row_first, own_rows, 0)
     own_len = lax.dynamic_slice_in_dim(lengths, row_first, own_rows, 0)
     visible = (first_key + jnp.arange(key_count, dtype=jnp.int32))[None, :] < own_len[:, None]

time: 376 us -> 485 us (1.29)
  waiting for transfers between devices: 232 us -> 330 us
  other arithmetic: 6.2 us -> 18.6 us
    all_gather x0 -> x1, waiting for transfers between devices: none -> 151 us  [on_device(): summed_mass = jnp.sum(lax.all_gather(partial_mass, 'heads'), axis=0)]
    psum x1 -> x0, waiting for transfers between devices: 53.3 us -> none  [on_device(): summed_mass = lax.psum(partial_mass, 'heads')]
    reduce_sum x0 -> x1, other arithmetic: none -> 11.8 us  [on_device(): summed_mass = jnp.sum(lax.all_gather(partial_mass, 'heads'), axis=0)]
  transfers between devices with their start and end apart: 4 -> 4, of which waited for: 4 -> 4; matrix products, arithmetic and copies ran while one was open for 7% -> 5% of each run, Pallas kernels for 0% -> 0%
where the time goes in v1:
time: 485 us; the launch traced here: 484 us
  waiting for transfers between devices  330 us (68%)
  blocking collectives  53.5 us (11%)
  matrix products  46.4 us (10%)
  local copies, waits for them, and re-layouts  21.6 us (4%)
  other arithmetic  18.6 us (4%)
  between operations  13.9 us (3%)
    all_gather x1, waiting for transfers between devices, on_device(): summed_mass = jnp.sum(lax.all_gather(partial_mass, 'heads'), axis=0)  151 us
    reduce_scatter x1, waiting for transfers between devices, on_device(): lax.psum_scatter(key_grad, 'heads', scatter_dimension=0, tiled=True)  79.8 us
    reduce_scatter x1, waiting for transfers between devices, on_device(): lax.psum_scatter(query_grad, 'context', scatter_dimension=1, tiled=True)  54.1 us
    all_gather x1, waiting for transfers between devices, on_device(): lax.all_gather(main_query, 'context', axis=0, tiled=True)  43.3 us
    psum x1, blocking collectives, on_device(): lax.psum((jnp.sum(weights_exp, axis=1), mass_local), 'context')  26.8 us
    pmax x1, blocking collectives, on_device(): top = lax.pmax(local_top, 'context')  26.7 us
    dot_general x4, matrix products, one_block(): jnp.einsum('rhd,sd->rhs', query_block, latent, preferred_element_type=jnp...  18.9 us
    dot_general x8, matrix products, block_dots(): lax.dot_general(flat_query, key_block, (((1,), (1,)), ((), ())), preferre...  15.6 us
  transfers between devices with their start and end apart: 4, of which 4 were waited for; matrix products, arithmetic and copies ran while one was open for 5% of the time, Pallas kernels for 0%

profile of v1, /device:TPU:2, one launch (start us, length us, event | category | flops | bytes accessed | tf_op | source)
XLA Modules:
  0.0 484.1 jit_solution(8940112433173455282)
XLA Ops:
  7.2 0.7 all-gather.3.cloned.1.call-update
  8.0 0.8 copy.24
  8.8 0.8 reshape.136
  9.6 43.3 %all-gather.3.cloned.1.call-done = bf16[256,8,576]{2,1,0:T(8,128)(2,1)} async-done(((bf16[16,8,576]{2,1,0:T(8,128)(2,1)}), bf16[256,8,576]{2,1,0:T(8,128)(2,1)}) %all-gather.3.cloned.1.call-update) | async-done | bytes 2359312 | tf_op jit(solution)/shard_map/all_gather | solution.py:44
  52.9 22.7 %while.36 = (s32[]{:T(128)}, f32[4,64,2048]{2,1,0:T(8,128)}, s32[4,64]{1,0:T(4,128)S(1)}, bf16[4,64,8,576]{3,2,1,0:T(8,128)(2,1)}, bf16[2048,576]{0,1:T(8,128)(2...) while((s32[]{:T(128)}, f32[4,64,2048]{2,1,0:T(8,128)}, s32[4,64]{1,0:T(4,128)S(1)}, ...), condition=%wide.region_8.9_spmd.clone, body=%wide.region_6.8_spmd.clone.sunk | while | flops 1211238400 | bytes 4611937 | solution.py:27
  52.9 4.7 exponential_reduce_fusion.2
  57.6 0.9 fusion.60
  58.5 4.7 exponential_reduce_fusion.2
  63.3 0.9 fusion.60
  64.2 4.7 exponential_reduce_fusion.2
  69.0 0.9 fusion.60
  69.9 4.7 exponential_reduce_fusion.2
  74.7 0.9 fusion.60
  75.7 0.6 copy-done.5
  76.4 0.2 copy-done
  76.5 0.2 copy-done.1
  76.7 20.1 %while.35 = (s32[]{:T(128)}, f32[4,16,512]{2,1,0:T(8,128)S(1)}, bf16[4,512,128]{2,1,0:T(8,128)(2,1)S(1)}, bf16[1024,128]{1,0:T(8,128)(2,1)S(1)}, f32[16,64]{1,0:T(8,128)S(1)}, /*index=5*/s32[]{:T(128)}) while((s32[]{:T(128)}, f32[4,16,512]{2,1,0:T(8,128)S(1)}, bf16[4,512,128]{2,1,0:T(8,128)(2,1)S(1)}, bf16[1024,128]{1,0:T(8,128)(2,1)S(1)}, ...), condition=%wide.region_1.2_spmd, body=%wide.region_0.1_spmd.sunk | while | flops 141041664 | bytes 8884301 | solution.py:79
  76.7 1.8 maximum_bitcast_fusion.2
  78.5 1.9 copy.40
  80.4 1.2 fusion.56
  81.7 1.8 maximum_bitcast_fusion.2
  83.5 1.9 copy.40
  85.4 1.2 fusion.56
  86.6 1.8 maximum_bitcast_fusion.2
  88.4 2.1 copy.40
  90.6 1.2 fusion.56
  91.8 1.8 maximum_bitcast_fusion.2
  93.6 1.9 copy.40
  95.6 1.2 fusion.56
  96.8 0.2 fusion.18
  97.0 26.7 %pmax.7 = f32[16]{0:T(128)S(1)} all-reduce(f32[16]{0:T(128)S(1)} %fusion.18), channel_id=1, replica_groups=mesh['context'=16,'heads'=16] {'context'}, use_global_device_ids=true, to_apply=%region_3.4 | all-reduce | flops 16 | bytes 128 | tf_op jit(solution)/shard_map/pmax | solution.py:82
  123.7 0.6 iota_add_fusion.1
  124.3 0.8 fusion.19
  125.1 151.2 %all-gather.5.cloned.1.call-done = f32[16,256,2048]{2,1,0:T(8,128)} async-done(((f32[1,256,2048]{2,1,0:T(8,128)}), f32[16,256,2048]{2,1,0:T(8,128)}) %all-gather.5.cloned.1.call-update) | async-done | bytes 33554448 | tf_op jit(solution)/shard_map/all_gather | solution.py:50
  276.3 11.8 %reduce_sum.39 = f32[256,2048]{1,0:T(8,128)S(1)} reduce(f32[16,256,2048]{2,1,0:T(8,128)} %all-gather.5.cloned.1.call-done, f32[]{:T(128)} %constant.44.clone.1), dimensions={0}, to_apply=%region_9.10 | reduce | flops 7864320 | bytes 35651588 | tf_op jit(solution)/shard_map/reduce_sum | solution.py:50
  288.1 0.7 dynamic-slice_reduce_fusion
  288.8 26.8 %all-reduce = (f32[16]{0:T(128)}, f32[16]{0:T(128)}) all-reduce(f32[16]{0:T(128)} %dynamic-slice_reduce_fusion, f32[16]{0:T(128)} %fusion.19), channel_id=1, replica_groups=mesh['context'=16,'heads'=16] {'context'}, use_global_device_ids=true, to_apply=%region_11.12 | all-reduce | flops 32 | bytes 256 | tf_op jit(solution)/shard_map/psum | solution.py:84
  315.6 0.8 subtract_multiply_fusion
  316.4 24.2 %while.37 = (s32[]{:T(128)}, f32[1024,128]{1,0:T(8,128)S(1)}, f32[4,512,128]{2,1,0:T(8,128)}, bf16[4,512,128]{2,1,0:T(8,128)(2,1)S(1)}, bf16[1024,128]{1,0:T(8,1...) while((s32[]{:T(128)}, f32[1024,128]{1,0:T(8,128)S(1)}, ...), condition=%wide.wide.region_13.14_spmd.clone, body=%wide.wide.region_12.13_spmd.clone.sunk | while | flops 405536768 | bytes 13734523 | solution.py:104
  316.4 0.3 mul.80
  316.7 1.9 copy.41
  318.6 2.1 select_convert_fusion.3
  320.7 0.6 convolution_add_fusion.3
  321.3 1.2 fusion.67
  322.5 0.3 mul.80
  322.7 1.9 copy.41
  324.6 2.1 select_convert_fusion.3
  326.7 0.6 convolution_add_fusion.3
  327.4 1.1 fusion.67
  328.5 0.3 mul.80
  328.8 1.9 copy.41
  330.6 2.1 select_convert_fusion.3
  332.7 0.6 convolution_add_fusion.3
  333.4 1.1 fusion.67
  334.5 0.3 mul.80
  334.8 1.9 copy.41
  336.7 2.1 select_convert_fusion.3
  338.8 0.6 convolution_add_fusion.3
  339.4 1.2 fusion.67
  340.6 1.1 copy.26
  341.7 0.5 reduce-scatter.5.cloned.1.call-update
  342.3 54.1 %reduce-scatter.3.cloned.1.call-done = f32[16,4,128]{2,0,1:T(8,128)} async-done(((f32[16,64,128]{2,0,1:T(8,128)}), f32[16,4,128]{2,0,1:T(8,128)}) %reduce-scatter.3.cloned.1.call-update) | async-done | bytes 32784 | tf_op jit(solution)/shard_map/reduce_scatter | solution.py:107
  396.4 1.4 copy.27
  397.8 79.8 %reduce-scatter.5.cloned.1.call-done = f32[128,128]{1,0:T(8,128)} async-done(((f32[2048,128]{1,0:T(8,128)}), f32[128,128]{1,0:T(8,128)}) %reduce-scatter.5.cloned.1.call-update) | async-done | bytes 65552 | tf_op jit(solution)/shard_map/reduce_scatter | solution.py:108
  (44 shorter events, 0.5 us)
Async XLA Ops:
  7.2 45.7 %all-gather.3.cloned.1.call-start = ((), (), s32[]{:S(2)}) async-start(), calls=%async_computation.2 | async-start | bytes 2785280 | tf_op jit(solution)/shard_map/all_gather | solution.py:44
  7.9 268.4 %all-gather.5.cloned.1.call-start = ((), (), s32[]{:S(2)}) async-start(), calls=%async_computation.3 | async-start | bytes 35651584 | tf_op jit(solution)/shard_map/all_gather | solution.py:50
  75.6 0.7 copy-start.5
  75.6 0.8 copy-start.2
  75.6 1.0 copy-start
  75.6 1.1 copy-start.1
  75.6 320.8 %reduce-scatter.3.cloned.1.call-start = ((), (), s32[]{:S(2)}) async-start(), calls=%async_computation.4 | async-start | bytes 557056 | tf_op jit(solution)/shard_map/reduce_scatter | solution.py:107
  123.7 1.4 copy-start.4
  125.1 190.5 %copy-start.3 = (s32[2048]{0:T(1024)S(1)}, s32[2048]{0:T(1024)}, u32[]{:S(2)}) copy-start(s32[2048]{0:T(1024)} %iota_add_fusion.1) | copy-start | bytes 24580
  341.7 135.9 %reduce-scatter.5.cloned.1.call-start = ((), (), s32[]{:S(2)}) async-start(), calls=%async_computation.5 | async-start | bytes 1114112 | tf_op jit(solution)/shard_map/reduce_scatter | solution.py:108
Sparse Core Ops, SparseCore 0:
  9.8 43.0 all-gather.2
  75.7 200.5 all-gather.4
  341.8 54.5 reduce-scatter.2
  400.3 77.2 reduce-scatter.4
